TPU v7x, 32 devices: a whole 2x2x4 slice. The times are simulated.
32 devices in a mesh: dp: 4 (over z), mp: 8 (over y, x, core).
Axes of the slice: x: 2, y: 2, z: 4, core: 2. Of those that a mesh axis runs over, the one named last changes fastest.
Arguments:
- features: bfloat16 [192, 1664], P('dp'), may hold values from -6 to 6
- output_grad: bfloat16 [192, 1664], P('dp'), may hold values from -6 to 6
- send_rows: int32 [16, 12], P('dp'), may hold values from 0 to 48, as said below
- patches: int32 [16], replicated, may hold values from 0 to 12, as said below
- up_weight: float32 [6144, 1664], P(('dp', 'mp'))
- down_weight: float32 [6144, 1664], P(('dp', 'mp'))
- up_moment: float32 [6144, 1664], P(('dp', 'mp')), may hold values from -0.0006 to 0.0006
- down_moment: float32 [6144, 1664], P(('dp', 'mp')), may hold values from -0.0006 to 0.0006
- up_second: float32 [6144, 1664], P(('dp', 'mp')), may hold values from 1e-09 to 1e-07
- down_second: float32 [6144, 1664], P(('dp', 'mp')), may hold values from 1e-09 to 1e-07
Outputs:
- new_up: float32 [6144, 1664], P(('dp', 'mp'))
- new_down: float32 [6144, 1664], P(('dp', 'mp'))
- ratios: float32 [2], replicated
Inputs may be any that keep to these rules, and one draw needn't show every extreme that they name: `send_rows`: row d * 4 + p lists the rows of group d's block sent to group p, one a slot, 48 marking an empty slot. Group d's live rows are the first ones of its block, as many as the sum of its 4 patch counts; each live row is listed exactly once in group d's rows and no other row is listed. In every draw some group fills all its slots. `patches`: entries d * 4 to d * 4 + 3 are the patch counts of group d's images, 0 for an empty place; in every draw some group's counts sum to 48.
All inputs are finite; a program needn't handle non-finite values.
Results may differ from a plain program's by a relative error of at most 0.0003.
Values may be sent and summed in bfloat16 or wider, within the bound.
No kernel may reach another device: no remote copies, remote signals or barrier semaphores. Data moves between devices by JAX's collectives and lax.ppermute only.
A program may use at most 64 MiB of HBM per device.

v0:
```python
import functools
import math

import jax
import jax.numpy as jnp
from jax import lax
from jax.experimental import pallas as pl
from jax.experimental.pallas import tpu as pltpu
from jax.sharding import PartitionSpec as P


inv_root_two = 1.0 / math.sqrt(2.0)
inv_root_tau = 1.0 / math.sqrt(2.0 * math.pi)
beta_first = 0.9
beta_second = 0.999
corr_first = 0.99997343860111
corr_second = 0.09520785288629
adam_eps = 1e-06
norm_eps = 1e-06
decay_rate = 0.05
learn_rate = 0.02


def gelu_exact(value):
    return 0.5 * value * (1.0 + lax.erf(value * inv_root_two))


def gelu_slope(value):
    return (
        0.5 * (1.0 + lax.erf(value * inv_root_two))
        + value * jnp.exp(-0.5 * value * value) * inv_root_tau
    )


def lamb_update(weight, grad, moment, second):
    moment_new = beta_first * moment + (1.0 - beta_first) * grad
    second_new = beta_second * second + (1.0 - beta_second) * grad * grad
    return (
        moment_new / corr_first / (jnp.sqrt(second_new / corr_second) + adam_eps)
        + decay_rate * weight
    )


def gather_weights(
    hidden_units,
    images,
    features,
    output_grad,
    send_rows,
    patches,
    up_weight,
    down_weight,
    up_moment,
    down_moment,
    up_second,
    down_second,
):
    width = features.shape[1]
    total = jnp.sum(patches).astype(jnp.float32)
    up_scale = 1.0 / math.sqrt(width)
    down_scale = 1.0 / math.sqrt(hidden_units)
    group = lax.axis_index("dp")
    counts = lax.dynamic_slice_in_dim(patches, group * images, images)
    live = jnp.sum(counts)
    inside = (jnp.arange(features.shape[0], dtype=jnp.int32) < live)[:, None]
    inputs = jnp.where(inside, features, jnp.zeros_like(features))
    cotangent = jnp.where(inside, output_grad, jnp.zeros_like(output_grad))
    stacked = jnp.stack([up_weight.astype(jnp.bfloat16), down_weight.astype(jnp.bfloat16)])
    piece = lax.all_gather(stacked, "dp", axis=1, tiled=True)
    pre_part = (
        lax.dot_general(
            inputs, piece[0], (((1,), (1,)), ((), ())), preferred_element_type=jnp.float32
        )
        * up_scale
    )
    back_part = (
        lax.dot_general(
            cotangent, piece[1], (((1,), (1,)), ((), ())), preferred_element_type=jnp.float32
        )
        * down_scale
    )
    both = jnp.stack([pre_part, back_part])
    pre = both[0]
    hidden = gelu_exact(pre).astype(jnp.bfloat16)
    slope = (both[1] * gelu_slope(pre)).astype(jnp.bfloat16)
    up_term = lax.dot_general(
        slope, inputs, (((0,), (0,)), ((), ())), preferred_element_type=jnp.float32
    ) * (up_scale / total)
    down_term = lax.dot_general(
        hidden, cotangent, (((0,), (0,)), ((), ())), preferred_element_type=jnp.float32
    ) * (down_scale / total)
    summed = lax.psum_scatter(
        jnp.concatenate([up_term, down_term], 1).astype(jnp.bfloat16),
        "dp",
        scatter_dimension=0,
        tiled=True,
    ).astype(jnp.float32)
    update_up = lamb_update(up_weight, summed[:, :width], up_moment, up_second)
    update_down = lamb_update(down_weight, summed[:, width:], down_moment, down_second)
    weight_up_sq, update_up_sq, weight_down_sq, update_down_sq = lax.psum(
        (
            jnp.sum(up_weight * up_weight),
            jnp.sum(update_up * update_up),
            jnp.sum(down_weight * down_weight),
            jnp.sum(update_down * update_down),
        ),
        ("dp", "mp"),
    )
    ratio_up = jnp.sqrt(weight_up_sq / (update_up_sq + norm_eps))
    ratio_down = jnp.sqrt(weight_down_sq / (update_down_sq + norm_eps))
    new_up = up_weight - learn_rate * ratio_up * update_up
    new_down = down_weight - learn_rate * ratio_down * update_down
    return (new_up, new_down, jnp.stack([ratio_up, ratio_down]))


moment_keep = beta_first / corr_first
moment_add = (1.0 - beta_first) / corr_first
second_keep = beta_second / corr_second
kernel_room = 16 * 2**20
second_add = (1.0 - beta_second) / corr_second


def column_chunks(width):
    edges = list(range(0, width, 256)) + [width]
    return list(zip(edges[:-1], edges[1:]))


def fold_rows(block):
    rows, columns = block.shape
    part = jnp.sum(block.reshape(rows // 8, 8, columns), axis=0)
    out = part[:, :128]
    for at in range(128, columns, 128):
        out = out + part[:, at : at + 128]
    return out


def prepare_kernel(*refs):
    sources, held = refs[:6], refs[6:12]
    halves, squares_ref, sem_ref = refs[12:14], refs[14], refs[15]
    copies = [
        pltpu.make_async_copy(source, target, sem_ref.at[at])
        for at, (source, target) in enumerate(zip(sources, held))
    ]
    for copy in copies:
        copy.start()
    for at in range(2):
        copies[at].wait()
        acc = jnp.zeros((8, 128), jnp.float32)
        for low, high in column_chunks(held[at].shape[1]):
            block = held[at][:, low:high]
            halves[at][:, low:high] = block.astype(jnp.bfloat16)
            acc = acc + fold_rows(block * block)
        squares_ref[at] = acc
    for copy in copies[2:]:
        copy.wait()


def update_kernel(groups, devices, hidden_units, *refs):
    patches_ref, squares_ref, features_ref, grads_ref = refs[:4]
    moved = refs[4 : 4 + 2 * (groups - 1)]
    (
        up_half_ref,
        down_half_ref,
        up_ref,
        down_ref,
        up_moment_ref,
        down_moment_ref,
        up_second_ref,
        down_second_ref,
        step_up_ref,
        step_down_ref,
        sums_ref,
        inputs_ref,
        cotangent_ref,
    ) = refs[4 + 2 * (groups - 1) :]
    cap, width = features_ref.shape
    tokens = groups * cap
    images = patches_ref.shape[0] // groups
    mine = lax.axis_index("dp")
    core = lax.rem(lax.axis_index("mp"), 2)
    up_scale = 1.0 / math.sqrt(width)
    down_scale = 1.0 / math.sqrt(hidden_units)

    inputs_ref[0:cap, :] = features_ref[...]
    cotangent_ref[0:cap, :] = grads_ref[...]
    for slot in range(1, groups):
        far, near = moved[slot - 1], moved[groups - 1 + slot - 1]
        rows = slice(slot * cap, (slot + 1) * cap)

        @pl.when(core == 0)
        def _():
            inputs_ref[rows, :] = far[...]
            cotangent_ref[rows, :] = near[...]

        @pl.when(core != 0)
        def _():
            inputs_ref[rows, :] = near[...]
            cotangent_ref[rows, :] = far[...]

    total = patches_ref[0]
    for at in range(1, groups * images):
        total = total + patches_ref[at]
    column = lax.broadcasted_iota(jnp.int32, (1, tokens), 1)
    alive = column < 0
    for slot in range(groups):
        group = lax.rem(mine - slot + groups, groups)
        live = patches_ref[group * images]
        for at in range(1, images):
            live = live + patches_ref[group * images + at]
        alive = alive | ((column >= slot * cap) & (column < slot * cap + live))

    across = (((1,), (1,)), ((), ()))
    pre = (
        lax.dot_general(
            up_half_ref[...], inputs_ref[...], across, preferred_element_type=jnp.float32
        )
        * up_scale
    )
    back = (
        lax.dot_general(
            down_half_ref[...], cotangent_ref[...], across, preferred_element_type=jnp.float32
        )
        * down_scale
    )
    half_erf = 0.5 * (1.0 + lax.erf(pre * inv_root_two))
    hidden = jnp.where(alive, pre * half_erf, 0.0).astype(jnp.bfloat16)
    tail = pre * jnp.exp(-0.5 * pre * pre) * inv_root_tau
    slope = jnp.where(alive, back * (half_erf + tail), 0.0).astype(jnp.bfloat16)

    spread = jnp.full((8, 128), total.astype(jnp.float32))
    parts = []
    for scale, left, right_ref, weight_ref, moment_ref, second_ref, step_ref in (
        (up_scale, slope, inputs_ref, up_ref, up_moment_ref, up_second_ref, step_up_ref),
        (
            down_scale,
            hidden,
            cotangent_ref,
            down_ref,
            down_moment_ref,
            down_second_ref,
            step_down_ref,
        ),
    ):
        factor = (scale / spread)[0:1, 0:1]
        acc = jnp.zeros((8, 128), jnp.float32)
        for low, high in column_chunks(width):
            grad = (
                jnp.dot(left, right_ref[:, low:high], preferred_element_type=jnp.float32)
                * factor
            )
            moment = moment_keep * moment_ref[:, low:high] + moment_add * grad
            second = second_keep * second_ref[:, low:high] + second_add * grad * grad
            step = (
                moment / (jnp.sqrt(second) + adam_eps) + decay_rate * weight_ref[:, low:high]
            )
            step_ref[:, low:high] = step
            acc = acc + fold_rows(step * step)
        parts.append(acc)
    lane = lax.broadcasted_iota(jnp.int32, (1, 128), 1)
    row = jnp.zeros((1, 128), jnp.float32)
    for at, value in enumerate((squares_ref[0], parts[0], squares_ref[1], parts[1])):
        one = jnp.sum(jnp.sum(value, axis=0, keepdims=True), axis=1, keepdims=True)
        row = jnp.where(lane == at, one, row)
    sums_ref[...] = jnp.broadcast_to(row, (devices, 128))


def finish_kernel(
    sums_ref,
    up_ref,
    down_ref,
    step_up_ref,
    step_down_ref,
    new_up_ref,
    new_down_ref,
    ratios_ref,
    held_ref,
    sem_ref,
):
    sums = jnp.sum(sums_ref[...], axis=0, keepdims=True)
    copies = []
    for at, (weight_ref, step_ref, new_ref) in enumerate(
        ((up_ref, step_up_ref, new_up_ref), (down_ref, step_down_ref, new_down_ref))
    ):
        ratio = jnp.sqrt(
            sums[:, 2 * at : 2 * at + 1] / (sums[:, 2 * at + 1 : 2 * at + 2] + norm_eps)
        )
        ratios_ref[at] = ratio[0, 0]
        rows = weight_ref.shape[0]
        cut = rows // 2
        for half, low in enumerate(range(0, rows, cut)):
            held_ref[at, low : low + cut, :] = (
                weight_ref[low : low + cut, :]
                - (learn_rate * ratio) * step_ref[low : low + cut, :]
            )
            copy = pltpu.make_async_copy(
                held_ref.at[at, low : low + cut],
                new_ref.at[low : low + cut],
                sem_ref.at[at, half],
            )
            copy.start()
            copies.append(copy)
    for copy in copies:
        copy.wait()


def keep_near(value):
    return pltpu.with_memory_space_constraint(value, pltpu.VMEM)


def gather_tokens(
    groups,
    members,
    hidden_units,
    features,
    output_grad,
    send_rows,
    patches,
    up_weight,
    down_weight,
    up_moment,
    down_moment,
    up_second,
    down_second,
):
    rows, width = up_weight.shape
    cap = features.shape[0]
    devices = groups * members
    vmem = pl.BlockSpec(memory_space=pltpu.VMEM)
    smem = pl.BlockSpec(memory_space=pltpu.SMEM)
    hbm = pl.BlockSpec(memory_space=pltpu.HBM)
    core = lax.axis_index("mp") % 2
    piece = jnp.where(core == 0, features, output_grad)
    far = []
    for slot in range(1, groups):
        ring = [(at, (at + slot) % groups) for at in range(groups)]
        far.append(lax.ppermute(piece, "dp", ring))
    pair = [(at, at ^ 1) for at in range(members)]
    near = [lax.ppermute(block, "mp", pair) for block in far]

    far = [keep_near(block) for block in far]
    near = [keep_near(block) for block in near]
    half = pltpu.VMEM((rows, width), jnp.bfloat16)
    held = pltpu.VMEM((rows, width), jnp.float32)
    weights = (up_weight, down_weight, up_moment, down_moment, up_second, down_second)
    prepare = pl.pallas_call(
        prepare_kernel,
        out_shape=(held,) * 6 + (half, half, pltpu.VMEM((2, 8, 128), jnp.float32)),
        in_specs=[hbm] * 6,
        out_specs=[vmem] * 9,
        scratch_shapes=[pltpu.SemaphoreType.DMA((6,))],
        compiler_params=pltpu.CompilerParams(vmem_limit_bytes=kernel_room),
        name="prepare",
    )
    *state, up_half, down_half, squares = prepare(
        *(pltpu.with_memory_space_constraint(value, pltpu.HBM) for value in weights)
    )
    step_up, step_down, sums = pl.pallas_call(
        functools.partial(update_kernel, groups, devices, hidden_units),
        out_shape=(held, held, pltpu.VMEM((devices, 128), jnp.float32)),
        in_specs=[smem] + [vmem] * (3 + 2 * (groups - 1) + 8),
        out_specs=[vmem] * 3,
        scratch_shapes=[
            pltpu.VMEM((groups * cap, width), jnp.bfloat16),
            pltpu.VMEM((groups * cap, width), jnp.bfloat16),
        ],
        compiler_params=pltpu.CompilerParams(vmem_limit_bytes=kernel_room),
        name="update",
    )(patches, squares, features, output_grad, *far, *near, up_half, down_half, *state)
    sums = keep_near(lax.all_to_all(sums, ("dp", "mp"), 0, 0, tiled=True))
    full = jax.ShapeDtypeStruct((rows, width), jnp.float32)
    return pl.pallas_call(
        finish_kernel,
        out_shape=(full, full, jax.ShapeDtypeStruct((2,), jnp.float32)),
        in_specs=[vmem] * 5,
        out_specs=[hbm, hbm, smem],
        scratch_shapes=[
            pltpu.VMEM((2, rows, width), jnp.float32),
            pltpu.SemaphoreType.DMA((2, 2)),
        ],
        compiler_params=pltpu.CompilerParams(vmem_limit_bytes=kernel_room),
        name="finish",
    )(sums, state[0], state[1], step_up, step_down)


def solution(mesh):
    groups, members = mesh.shape["dp"], mesh.shape["mp"]
    spread = P(("dp", "mp"), None)
    placed = (P("dp", None), P("dp", None), P("dp", None), P()) + (spread,) * 6

    def use_tokens(tokens, hidden_units):
        return members % 2 == 0 and tokens <= hidden_units // members

    def whole(features, output_grad, send_rows, patches, up_weight, *others):
        hidden_units, _ = up_weight.shape
        tokens = features.shape[0]
        if use_tokens(tokens, hidden_units):
            body = functools.partial(gather_tokens, groups, members, hidden_units)
        else:
            body = functools.partial(gather_weights, hidden_units, patches.shape[0] // groups)
        step = jax.shard_map(
            body,
            mesh=mesh,
            in_specs=placed,
            out_specs=(spread, spread, P()),
            check_vma=False,
        )
        return step(features, output_grad, send_rows, patches, up_weight, *others)

    return whole
```

profile of v0, /device:TPU:0, one launch (start us, length us, event | category | flops | bytes accessed | tf_op | source)
XLA Modules:
  0.0 41.4 jit_solution(6989173127894324154)
XLA Ops:
  0.6 0.9 %broadcast_select_fusion = bf16[48,1664]{1,0:T(8,128)(2,1)S(1)} fusion(bf16[48,1664]{1,0:T(8,128)(2,1)} %refs_2_.3, bf16[48,1664]{1,0:T(8,128)(2,1)} %refs_3_.3, pred[]{:T(512)S(6)} %eq.5), kind=kLoop, calls=%fused_computation | loop fusion | flops 79872 | bytes 479233 | tf_op jit(solution)/shard_map/jit(_where)/select_n | solution.py:332
  1.6 0.0 copy-start
  1.6 0.0 copy-start.1
  1.6 0.0 copy-start.2
  1.6 5.1 %collective-permute-start.2 = (bf16[48,1664]{1,0:T(8,128)(2,1)S(1)}, bf16[48,1664]{1,0:T(8,128)(2,1)S(1)}, u32[]{:S(2)}, u32[]{:S(2)}) collective-permute-start(bf16[48,1664]{1,0:T(8,128)(2,1)S(1)} %broadcast_select_fusion), channel_id=1, source_target_pairs={{0,24},{8,0},{16,8},{24,16},{1,25},{9,1},{17,9},{25,17},{2,26},{10... | collective-permute-start | bytes 479240 | tf_op jit(solution)/shard_map/ppermute | solution.py:336
  6.8 0.0 collective-permute-start.1
  6.8 1.0 %collective-permute-start = (bf16[48,1664]{1,0:T(8,128)(2,1)S(1)}, bf16[48,1664]{1,0:T(8,128)(2,1)S(1)}, u32[]{:S(2)}, u32[]{:S(2)}) collective-permute-start(bf16[48,1664]{1,0:T(8,128)(2,1)S(1)} %broadcast_select_fusion), channel_id=1, source_target_pairs={{0,8},{8,16},{16,24},{24,0},{1,9},{9,17},{17,25},{25,1},{2,10},{10... | collective-permute-start | bytes 479240 | tf_op jit(solution)/shard_map/ppermute | solution.py:336
  7.8 3.5 %collective-permute-done.2.refs_6_ = bf16[48,1664]{1,0:T(8,128)(2,1)S(1)} collective-permute-done((bf16[48,1664]{1,0:T(8,128)(2,1)S(1)}, bf16[48,1664]{1,0:T(8,128)(2,1)S(1)}, u32[]{:S(2)}, u32[]{:S(2)}) %collective-permute-start.2) | collective-permute-done | bytes 159776 | tf_op jit(solution)/shard_map/ppermute | solution.py:336
  11.3 0.0 collective-permute-start.5
  11.3 9.0 %collective-permute-done.1.refs_5_ = bf16[48,1664]{1,0:T(8,128)(2,1)S(1)} collective-permute-done((bf16[48,1664]{1,0:T(8,128)(2,1)S(1)}, bf16[48,1664]{1,0:T(8,128)(2,1)S(1)}, u32[]{:S(2)}, u32[]{:S(2)}) %collective-permute-start.1) | collective-permute-done | bytes 159776 | tf_op jit(solution)/shard_map/ppermute | solution.py:336
  20.3 0.0 collective-permute-start.4
  20.3 0.0 collective-permute-done.refs_4_
  20.3 0.5 %collective-permute-start.3 = (bf16[48,1664]{1,0:T(8,128)(2,1)S(1)}, bf16[48,1664]{1,0:T(8,128)(2,1)S(1)}, u32[]{:S(2)}, u32[]{:S(2)}) collective-permute-start(bf16[48,1664]{1,0:T(8,128)(2,1)S(1)} %collective-permute-done.refs_4_), channel_id=1, source_target_pairs={{0,1},{1,0},{2,3},{3,2},{4,5},{5,4},{6,7},{7,6},{8,9},{9,8},{10,11... | collective-permute-start | bytes 479240 | tf_op jit(solution)/shard_map/ppermute | solution.py:338
  20.8 3.3 %prepare.1 = (f32[192,1664]{1,0:T(8,128)S(1)}, f32[192,1664]{1,0:T(8,128)S(1)}, f32[192,1664]{1,0:T(8,128)S(1)}, f32[192,1664]{1,0:T(8,128)S(1)}, f32[192,1664]{...) custom-call(f32[192,1664]{1,0:T(8,128)} %refs_0_.2, ...), custom_call_target="tpu_custom_call" | custom-call | tf_op jit(solution)/shard_map/prepare/pallas_call | solution.py:354
  24.1 0.0 collective-permute-done.5.refs_9_
  24.1 0.0 collective-permute-done.4.refs_8_
  24.1 0.0 collective-permute-done.3.refs_7_
  24.1 0.0 copy-done
  24.1 0.0 copy-done.1
  24.1 0.0 copy-done.2
  24.1 3.4 %update.1 = (f32[192,1664]{1,0:T(8,128)S(1)}, f32[192,1664]{1,0:T(8,128)S(1)}, f32[32,128]{1,0:T(8,128)S(1)}) custom-call(s32[16]{0:T(128)S(1)} %copy-done.2, f32[2,8,128]{2,1,0:T(8,128)S(1)} %get-tuple-element.15.refs_1_, bf16[48,1664]{1,0:T(8,128)(2,1)S(1)} %copy-done, bf16[48,1664]{1,0:T(8,128)(2,1)S(1)} %copy-done.1, ...), custom_call_target="tpu_custom_call" | custom-call | tf_op jit(solution)/shard_map/update/pallas_call | solution.py:357
  27.6 11.6 %all_to_all.11 = f32[32,1,128]{2,1,0:T(1,128)S(1)} all-to-all(f32[32,1,128]{2,1,0:T(1,128)S(1)} %bitcast.5), channel_id=1, replica_groups=mesh['dp'=4,'mp'=8] {'dp','mp'}, dimensions={0} | all-to-all | bytes 32768 | tf_op jit(solution)/shard_map/all_to_all | solution.py:369
  39.2 2.2 %finish.1 = (f32[192,1664]{1,0:T(8,128)}, f32[192,1664]{1,0:T(8,128)}, f32[2]{0:T(128)}) custom-call(f32[32,128]{1,0:T(8,128)S(1)} %bitcast.4, f32[192,1664]{1,0:T(8,128)S(1)} %get-tuple-element.18.refs_12_.up_ref, f32[192,1664]{1,0:T(8,128)S(1)} %get-tuple-element.19.refs_13_.down_ref, f32[192,1664]{1,0:T(8,128)S(1)} %get-tuple-element.25.step_up_ref, ...), custom_call_target="tpu_custom_call" | custom-call | tf_op jit(solution)/shard_map/finish/pallas_call | solution.py:371
Async XLA Ops:
  1.6 22.5 %copy-start = (bf16[48,1664]{1,0:T(8,128)(2,1)S(1)}, bf16[48,1664]{1,0:T(8,128)(2,1)}, u32[]{:S(2)}) copy-start(bf16[48,1664]{1,0:T(8,128)(2,1)} %refs_2_.3) | copy-start | bytes 479236
  1.6 22.5 %copy-start.1 = (bf16[48,1664]{1,0:T(8,128)(2,1)S(1)}, bf16[48,1664]{1,0:T(8,128)(2,1)}, u32[]{:S(2)}) copy-start(bf16[48,1664]{1,0:T(8,128)(2,1)} %refs_3_.3) | copy-start | bytes 479236
  1.6 22.5 %copy-start.2 = (s32[16]{0:T(128)S(1)}, s32[16]{0:T(128)}, u32[]{:S(2)}) copy-start(s32[16]{0:T(128)} %refs_0_.3) | copy-start | bytes 196
  1.6 9.7 %collective-permute-start.2 = (bf16[48,1664]{1,0:T(8,128)(2,1)S(1)}, bf16[48,1664]{1,0:T(8,128)(2,1)S(1)}, u32[]{:S(2)}, u32[]{:S(2)}) collective-permute-start(bf16[48,1664]{1,0:T(8,128)(2,1)S(1)} %broadcast_select_fusion), channel_id=1, source_target_pairs={{0,24},{8,0},{16,8},{24,16},{1,25},{9,1},{17,9},{25,17},{2,26},{10... | collective-permute-start | bytes 479240 | tf_op jit(solution)/shard_map/ppermute | solution.py:336
  6.8 13.5 %collective-permute-start.1 = (bf16[48,1664]{1,0:T(8,128)(2,1)S(1)}, bf16[48,1664]{1,0:T(8,128)(2,1)S(1)}, u32[]{:S(2)}, u32[]{:S(2)}) collective-permute-start(bf16[48,1664]{1,0:T(8,128)(2,1)S(1)} %broadcast_select_fusion), channel_id=1, source_target_pairs={{0,16},{8,24},{16,0},{24,8},{1,17},{9,25},{17,1},{25,9},{2,18},{10... | collective-permute-start | bytes 479240 | tf_op jit(solution)/shard_map/ppermute | solution.py:336
  6.8 13.5 %collective-permute-start = (bf16[48,1664]{1,0:T(8,128)(2,1)S(1)}, bf16[48,1664]{1,0:T(8,128)(2,1)S(1)}, u32[]{:S(2)}, u32[]{:S(2)}) collective-permute-start(bf16[48,1664]{1,0:T(8,128)(2,1)S(1)} %broadcast_select_fusion), channel_id=1, source_target_pairs={{0,8},{8,16},{16,24},{24,0},{1,9},{9,17},{17,25},{25,1},{2,10},{10... | collective-permute-start | bytes 479240 | tf_op jit(solution)/shard_map/ppermute | solution.py:336
  11.3 12.8 %collective-permute-start.5 = (bf16[48,1664]{1,0:T(8,128)(2,1)S(1)}, bf16[48,1664]{1,0:T(8,128)(2,1)S(1)}, u32[]{:S(2)}, u32[]{:S(2)}) collective-permute-start(bf16[48,1664]{1,0:T(8,128)(2,1)S(1)} %collective-permute-done.2.refs_6_), channel_id=1, source_target_pairs={{0,1},{1,0},{2,3},{3,2},{4,5},{5,4},{6,7},{7,6},{8,9},{9,8},{10,11... | collective-permute-start | bytes 479240 | tf_op jit(solution)/shard_map/ppermute | solution.py:338
  20.3 3.8 %collective-permute-start.4 = (bf16[48,1664]{1,0:T(8,128)(2,1)S(1)}, bf16[48,1664]{1,0:T(8,128)(2,1)S(1)}, u32[]{:S(2)}, u32[]{:S(2)}) collective-permute-start(bf16[48,1664]{1,0:T(8,128)(2,1)S(1)} %collective-permute-done.1.refs_5_), channel_id=1, source_target_pairs={{0,1},{1,0},{2,3},{3,2},{4,5},{5,4},{6,7},{7,6},{8,9},{9,8},{10,11... | collective-permute-start | bytes 479240 | tf_op jit(solution)/shard_map/ppermute | solution.py:338
  20.3 3.8 %collective-permute-start.3 = (bf16[48,1664]{1,0:T(8,128)(2,1)S(1)}, bf16[48,1664]{1,0:T(8,128)(2,1)S(1)}, u32[]{:S(2)}, u32[]{:S(2)}) collective-permute-start(bf16[48,1664]{1,0:T(8,128)(2,1)S(1)} %collective-permute-done.refs_4_), channel_id=1, source_target_pairs={{0,1},{1,0},{2,3},{3,2},{4,5},{5,4},{6,7},{7,6},{8,9},{9,8},{10,11... | collective-permute-start | bytes 479240 | tf_op jit(solution)/shard_map/ppermute | solution.py:338
where the time goes:
time: 41.6 us; the launch traced here: 41.4 us
  waiting for transfers between devices  12.5 us (30%)
  blocking collectives  11.6 us (28%)
  Pallas kernels  8.93 us (21%)
  starting transfers between devices  6.66 us (16%)
  other arithmetic  0.95 us (2%)
  between operations  0.73 us (2%)
    ppermute x3, waiting for transfers between devices, gather_tokens(): far.append(lax.ppermute(piece, 'dp', ring))  12.5 us
    all_to_all x1, blocking collectives, gather_tokens(): sums = keep_near(lax.all_to_all(sums, ('dp', 'mp'), 0, 0, tiled=True))  11.6 us
    ppermute x3, starting transfers between devices, gather_tokens(): far.append(lax.ppermute(piece, 'dp', ring))  6.14 us
    pallas_call x1, Pallas kernels, gather_tokens(): pl.pallas_call(functools.partial(update_kernel, groups, devices, hidden_u...  3.43 us
    pallas_call x1, Pallas kernels, gather_tokens(): prepare(*(pltpu.with_memory_space_constraint(value, pltpu.HBM) for value...  3.26 us
    pallas_call x1, Pallas kernels, gather_tokens(): pl.pallas_call(finish_kernel, out_shape=(full, full, jax.ShapeDtypeStruct...  2.24 us
    select_n x1, other arithmetic, gather_tokens(): piece = jnp.where(core == 0, features, output_grad)  0.95 us
  transfers between devices with their start and end apart: 6, of which 2 were waited for; matrix products, arithmetic and copies ran while one was open for 0% of the time, Pallas kernels for 8%

commit v1 on v0

--- a/solution.py
+++ b/solution.py
@@ -135,11 +135,12 @@
 
 
 def prepare_kernel(*refs):
-    sources, held = refs[:6], refs[6:12]
-    halves, squares_ref, sem_ref = refs[12:14], refs[14], refs[15]
+    sources, held = refs[:6], refs[6:8]
+    halves, scaled, squares_ref = refs[8:10], refs[10:16], refs[16]
+    raw, sem_ref = refs[17:21], refs[21]
     copies = [
         pltpu.make_async_copy(source, target, sem_ref.at[at])
-        for at, (source, target) in enumerate(zip(sources, held))
+        for at, (source, target) in enumerate(zip(sources, (*held, *raw)))
     ]
     for copy in copies:
         copy.start()
@@ -149,15 +150,19 @@
         for low, high in column_chunks(held[at].shape[1]):
             block = held[at][:, low:high]
             halves[at][:, low:high] = block.astype(jnp.bfloat16)
+            scaled[at][:, low:high] = decay_rate * block
             acc = acc + fold_rows(block * block)
         squares_ref[at] = acc
-    for copy in copies[2:]:
-        copy.wait()
+    for at in range(4):
+        copies[2 + at].wait()
+        keep = moment_keep if at < 2 else second_keep
+        scaled[2 + at][...] = keep * raw[at][...]
 
 
 def update_kernel(groups, devices, hidden_units, *refs):
     patches_ref, squares_ref, features_ref, grads_ref = refs[:4]
-    moved = refs[4 : 4 + 2 * (groups - 1)]
+    pieces = piece_list(groups)
+    moved = refs[4 : 4 + 2 * len(pieces)]
     (
         up_half_ref,
         down_half_ref,
@@ -172,7 +177,7 @@
         sums_ref,
         inputs_ref,
         cotangent_ref,
-    ) = refs[4 + 2 * (groups - 1) :]
+    ) = refs[4 + 2 * len(pieces) :]
     cap, width = features_ref.shape
     tokens = groups * cap
     images = patches_ref.shape[0] // groups
@@ -183,9 +188,10 @@
 
     inputs_ref[0:cap, :] = features_ref[...]
     cotangent_ref[0:cap, :] = grads_ref[...]
-    for slot in range(1, groups):
-        far, near = moved[slot - 1], moved[groups - 1 + slot - 1]
-        rows = slice(slot * cap, (slot + 1) * cap)
+    for at, (slot, half) in enumerate(pieces):
+        far, near = moved[at], moved[len(pieces) + at]
+        low = slot * cap + half * (cap // 2)
+        rows = slice(low, low + far.shape[0])
 
         @pl.when(core == 0)
         def _():
@@ -203,11 +209,18 @@
     column = lax.broadcasted_iota(jnp.int32, (1, tokens), 1)
     alive = column < 0
     for slot in range(groups):
-        group = lax.rem(mine - slot + groups, groups)
+        group = lax.bitwise_xor(mine, slot)
         live = patches_ref[group * images]
         for at in range(1, images):
             live = live + patches_ref[group * images + at]
-        alive = alive | ((column >= slot * cap) & (column < slot * cap + live))
+        place = column - slot * cap
+        stride = swap_stride(groups, slot) if slot else 0
+        if stride:
+            shift = lax.rem(lax.div(lax.axis_index("mp"), stride), 2) * (cap // 2)
+            row = place + jnp.where(place < cap // 2, shift, -shift)
+        else:
+            row = place
+        alive = alive | ((place >= 0) & (place < cap) & (row < live))
 
     across = (((1,), (1,)), ((), ()))
     pre = (
@@ -242,17 +255,14 @@
         ),
     ):
         factor = (scale / spread)[0:1, 0:1]
+        moment_factor, second_factor = moment_add * factor, math.sqrt(second_add) * factor
         acc = jnp.zeros((8, 128), jnp.float32)
         for low, high in column_chunks(width):
-            grad = (
-                jnp.dot(left, right_ref[:, low:high], preferred_element_type=jnp.float32)
-                * factor
-            )
-            moment = moment_keep * moment_ref[:, low:high] + moment_add * grad
-            second = second_keep * second_ref[:, low:high] + second_add * grad * grad
-            step = (
-                moment / (jnp.sqrt(second) + adam_eps) + decay_rate * weight_ref[:, low:high]
-            )
+            grad = jnp.dot(left, right_ref[:, low:high], preferred_element_type=jnp.float32)
+            moment = moment_ref[:, low:high] + grad * moment_factor
+            root = grad * second_factor
+            second = second_ref[:, low:high] + root * root
+            step = moment / (second * lax.rsqrt(second) + adam_eps) + weight_ref[:, low:high]
             step_ref[:, low:high] = step
             acc = acc + fold_rows(step * step)
         parts.append(acc)
@@ -274,9 +284,13 @@
     new_down_ref,
     ratios_ref,
     held_ref,
+    pair_ref,
     sem_ref,
+    pair_sem_ref,
 ):
     sums = jnp.sum(sums_ref[...], axis=0, keepdims=True)
+    rows = up_ref.shape[0]
+    cut = rows // sem_ref.shape[1]
     copies = []
     for at, (weight_ref, step_ref, new_ref) in enumerate(
         ((up_ref, step_up_ref, new_up_ref), (down_ref, step_down_ref, new_down_ref))
@@ -284,23 +298,37 @@
         ratio = jnp.sqrt(
             sums[:, 2 * at : 2 * at + 1] / (sums[:, 2 * at + 1 : 2 * at + 2] + norm_eps)
         )
-        ratios_ref[at] = ratio[0, 0]
-        rows = weight_ref.shape[0]
-        cut = rows // 2
-        for half, low in enumerate(range(0, rows, cut)):
-            held_ref[at, low : low + cut, :] = (
-                weight_ref[low : low + cut, :]
-                - (learn_rate * ratio) * step_ref[low : low + cut, :]
+        pair_ref[at] = ratio[0, 0]
+        for part in range(sem_ref.shape[1]):
+            here = pl.ds(part * cut, cut)
+            held_ref[at, here, :] = (
+                weight_ref[here, :] - (learn_rate * ratio) * step_ref[here, :]
             )
             copy = pltpu.make_async_copy(
-                held_ref.at[at, low : low + cut],
-                new_ref.at[low : low + cut],
-                sem_ref.at[at, half],
+                held_ref.at[at, here], new_ref.at[here], sem_ref.at[at, part]
             )
             copy.start()
             copies.append(copy)
+    copies.append(pltpu.make_async_copy(pair_ref, ratios_ref, pair_sem_ref))
+    copies[-1].start()
     for copy in copies:
         copy.wait()
+
+
+def swap_stride(groups, slot):
+    return 2 if slot == groups - 1 else 0
+
+
+def slot_order(groups):
+    return [groups - 1, *range(1, groups - 1)]
+
+
+def piece_list(groups):
+    return [
+        (slot, half)
+        for slot in slot_order(groups)
+        for half in range(2 if swap_stride(groups, slot) else 1)
+    ]
 
 
 def keep_near(value):
@@ -328,15 +356,24 @@
     vmem = pl.BlockSpec(memory_space=pltpu.VMEM)
     smem = pl.BlockSpec(memory_space=pltpu.SMEM)
     hbm = pl.BlockSpec(memory_space=pltpu.HBM)
-    core = lax.axis_index("mp") % 2
-    piece = jnp.where(core == 0, features, output_grad)
-    far = []
-    for slot in range(1, groups):
-        ring = [(at, (at + slot) % groups) for at in range(groups)]
-        far.append(lax.ppermute(piece, "dp", ring))
+    member = lax.axis_index("mp")
+    piece = jnp.where(member % 2 == 0, features, output_grad)
     pair = [(at, at ^ 1) for at in range(members)]
-    near = [lax.ppermute(block, "mp", pair) for block in far]
-
+    far, near = [], []
+    for slot in slot_order(groups):
+        stride = swap_stride(groups, slot)
+        sent = piece
+        if stride:
+            side = member // stride % 2
+            sent = lax.dynamic_slice_in_dim(piece, side * (cap // 2), cap // 2)
+        swap = [(at, at ^ slot) for at in range(groups)]
+        blocks = [lax.ppermute(sent, "dp", swap)]
+        if stride:
+            across = [(at, at ^ stride) for at in range(members)]
+            blocks.append(lax.ppermute(blocks[0], "mp", across))
+        for half, block in enumerate(blocks):
+            near.append(lax.ppermute(block, "mp", pair))
+            far.append(block)
     far = [keep_near(block) for block in far]
     near = [keep_near(block) for block in near]
     half = pltpu.VMEM((rows, width), jnp.bfloat16)
@@ -344,20 +381,20 @@
     weights = (up_weight, down_weight, up_moment, down_moment, up_second, down_second)
     prepare = pl.pallas_call(
         prepare_kernel,
-        out_shape=(held,) * 6 + (half, half, pltpu.VMEM((2, 8, 128), jnp.float32)),
+        out_shape=(held, held, half, half) + (held,) * 6 + (pltpu.VMEM((2, 8, 128), jnp.float32),),
         in_specs=[hbm] * 6,
-        out_specs=[vmem] * 9,
-        scratch_shapes=[pltpu.SemaphoreType.DMA((6,))],
+        out_specs=[vmem] * 11,
+        scratch_shapes=[held] * 4 + [pltpu.SemaphoreType.DMA((6,))],
         compiler_params=pltpu.CompilerParams(vmem_limit_bytes=kernel_room),
         name="prepare",
     )
-    *state, up_half, down_half, squares = prepare(
+    near_up, near_down, up_half, down_half, *scaled, squares = prepare(
         *(pltpu.with_memory_space_constraint(value, pltpu.HBM) for value in weights)
     )
     step_up, step_down, sums = pl.pallas_call(
         functools.partial(update_kernel, groups, devices, hidden_units),
         out_shape=(held, held, pltpu.VMEM((devices, 128), jnp.float32)),
-        in_specs=[smem] + [vmem] * (3 + 2 * (groups - 1) + 8),
+        in_specs=[smem] + [vmem] * (3 + 2 * len(far) + 8),
         out_specs=[vmem] * 3,
         scratch_shapes=[
             pltpu.VMEM((groups * cap, width), jnp.bfloat16),
@@ -365,21 +402,23 @@
         ],
         compiler_params=pltpu.CompilerParams(vmem_limit_bytes=kernel_room),
         name="update",
-    )(patches, squares, features, output_grad, *far, *near, up_half, down_half, *state)
+    )(patches, squares, features, output_grad, *far, *near, up_half, down_half, *scaled)
     sums = keep_near(lax.all_to_all(sums, ("dp", "mp"), 0, 0, tiled=True))
     full = jax.ShapeDtypeStruct((rows, width), jnp.float32)
     return pl.pallas_call(
         finish_kernel,
         out_shape=(full, full, jax.ShapeDtypeStruct((2,), jnp.float32)),
         in_specs=[vmem] * 5,
-        out_specs=[hbm, hbm, smem],
+        out_specs=[hbm] * 3,
         scratch_shapes=[
             pltpu.VMEM((2, rows, width), jnp.float32),
-            pltpu.SemaphoreType.DMA((2, 2)),
+            pltpu.SMEM((2,), jnp.float32),
+            pltpu.SemaphoreType.DMA((2, 6)),
+            pltpu.SemaphoreType.DMA,
         ],
         compiler_params=pltpu.CompilerParams(vmem_limit_bytes=kernel_room),
         name="finish",
-    )(sums, state[0], state[1], step_up, step_down)
+    )(sums, near_up, near_down, step_up, step_down)
 
 
 def solution(mesh):
@@ -388,7 +427,8 @@
     placed = (P("dp", None), P("dp", None), P("dp", None), P()) + (spread,) * 6
 
     def use_tokens(tokens, hidden_units):
-        return members % 2 == 0 and tokens <= hidden_units // members
+        paired = members % 4 == 0 and groups > 2 and groups & (groups - 1) == 0
+        return paired and tokens <= hidden_units // members
 
     def whole(features, output_grad, send_rows, patches, up_weight, *others):
         hidden_units, _ = up_weight.shape

time: 41.6 us -> 41 us (0.986)
  waiting for transfers between devices: 12.5 us -> 11.1 us
  Pallas kernels: 8.93 us -> 7.72 us
  starting transfers between devices: 6.66 us -> 7.85 us
  blocking collectives: 11.6 us -> 12.5 us
    ppermute x6 -> x8, waiting for transfers between devices: 12.5 us -> 11.1 us  [the longest x3 8.77 us: gather_tokens(): blocks = [lax.ppermute(sent, 'dp', swap)]]
    ppermute x6 -> x8, starting transfers between devices: 6.66 us -> 7.85 us  [the longest x3 5.78 us: gather_tokens(): blocks = [lax.ppermute(sent, 'dp', swap)]]
    all_to_all x1, blocking collectives: 11.6 us -> 12.5 us  [gather_tokens(): sums = keep_near(lax.all_to_all(sums, ('dp', 'mp'), 0, 0, tiled=True))]
    pallas_call x1, Pallas kernels: 3.43 us -> 2.61 us  [gather_tokens(): pl.pallas_call(functools.partial(update_kernel, groups, devices, hidden_u...]
    pallas_call x1, Pallas kernels: 2.24 us -> 1.73 us  [gather_tokens(): pl.pallas_call(finish_kernel, out_shape=(full, full, jax.ShapeDtypeStruct...]
  transfers between devices with their start and end apart: 6 -> 8, of which waited for: 2 -> 2; matrix products, arithmetic and copies ran while one was open for 0% -> 0% of each run, Pallas kernels for 8% -> 8%
where the time goes in v1:
time: 41 us; the launch traced here: 40.9 us
  blocking collectives  12.5 us (30%)
  waiting for transfers between devices  11.1 us (27%)
  starting transfers between devices  7.85 us (19%)
  Pallas kernels  7.72 us (19%)
  other arithmetic  0.95 us (2%)
  between operations  0.75 us (2%)
    all_to_all x1, blocking collectives, gather_tokens(): sums = keep_near(lax.all_to_all(sums, ('dp', 'mp'), 0, 0, tiled=True))  12.5 us
    ppermute x3, waiting for transfers between devices, gather_tokens(): blocks = [lax.ppermute(sent, 'dp', swap)]  8.77 us
    ppermute x3, starting transfers between devices, gather_tokens(): blocks = [lax.ppermute(sent, 'dp', swap)]  5.78 us
    pallas_call x1, Pallas kernels, gather_tokens(): prepare(*(pltpu.with_memory_space_constraint(value, pltpu.HBM) for value...  3.37 us
    pallas_call x1, Pallas kernels, gather_tokens(): pl.pallas_call(functools.partial(update_kernel, groups, devices, hidden_u...  2.61 us
    ppermute x1, waiting for transfers between devices, gather_tokens(): blocks.append(lax.ppermute(blocks[0], 'mp', across))  2.34 us
    pallas_call x1, Pallas kernels, gather_tokens(): pl.pallas_call(finish_kernel, out_shape=(full, full, jax.ShapeDtypeStruct...  1.73 us
    ppermute x1, starting transfers between devices, gather_tokens(): blocks.append(lax.ppermute(blocks[0], 'mp', across))  1.49 us
  transfers between devices with their start and end apart: 8, of which 2 were waited for; matrix products, arithmetic and copies ran while one was open for 0% of the time, Pallas kernels for 8%

profile of v1, /device:TPU:0, one launch (start us, length us, event | category | flops | bytes accessed | tf_op | source)
XLA Modules:
  0.0 40.9 jit_solution(2288249758449670780)
XLA Ops:
  0.6 0.9 %broadcast_select_fusion = bf16[48,1664]{1,0:T(8,128)(2,1)S(1)} fusion(bf16[48,1664]{1,0:T(8,128)(2,1)} %refs_2_.3, bf16[48,1664]{1,0:T(8,128)(2,1)} %refs_3_.3, pred[]{:T(512)S(6)} %eq.6), kind=kLoop, calls=%fused_computation | loop fusion | flops 79872 | bytes 479233 | tf_op jit(solution)/shard_map/jit(_where)/select_n | solution.py:360
  1.6 4.1 %collective-permute-start.3 = (bf16[48,1664]{1,0:T(8,128)(2,1)S(1)}, bf16[48,1664]{1,0:T(8,128)(2,1)S(1)}, u32[]{:S(2)}, u32[]{:S(2)}) collective-permute-start(bf16[48,1664]{1,0:T(8,128)(2,1)S(1)} %broadcast_select_fusion), channel_id=1, source_target_pairs={{0,16},{8,24},{16,0},{24,8},{1,17},{9,25},{17,1},{25,9},{2,18},{10... | collective-permute-start | bytes 479240 | tf_op jit(solution)/shard_map/ppermute | solution.py:370
  5.7 1.6 %collective-permute-start.2 = (bf16[48,1664]{1,0:T(8,128)(2,1)S(1)}, bf16[48,1664]{1,0:T(8,128)(2,1)S(1)}, u32[]{:S(2)}, u32[]{:S(2)}) collective-permute-start(bf16[48,1664]{1,0:T(8,128)(2,1)S(1)} %broadcast_select_fusion), channel_id=1, source_target_pairs={{0,8},{8,0},{16,24},{24,16},{1,9},{9,1},{17,25},{25,17},{2,10},{10... | collective-permute-start | bytes 479240 | tf_op jit(solution)/shard_map/ppermute | solution.py:370
  7.3 0.0 copy-start
  7.3 0.0 copy-start.1
  7.3 0.0 copy-start.2
  7.3 0.1 collective-permute-start
  7.4 8.8 %collective-permute-done.refs_4_ = bf16[24,1664]{1,0:T(8,128)(2,1)S(1)} collective-permute-done((bf16[24,1664]{1,0:T(8,128)(2,1)S(1)}, bf16[24,1664]{1,0:T(8,128)(2,1)S(1)}, u32[]{:S(2)}, u32[]{:S(2)}) %collective-permute-start) | collective-permute-done | bytes 79904 | tf_op jit(solution)/shard_map/ppermute | solution.py:370
  16.2 1.5 %collective-permute-start.1 = (bf16[24,1664]{1,0:T(8,128)(2,1)S(1)}, bf16[24,1664]{1,0:T(8,128)(2,1)S(1)}, u32[]{:S(2)}, u32[]{:S(2)}) collective-permute-start(bf16[24,1664]{1,0:T(8,128)(2,1)S(1)} %collective-permute-done.refs_4_), channel_id=1, source_target_pairs={{0,2},{1,3},{2,0},{3,1},{4,6},{5,7},{6,4},{7,5},{8,10},{9,11},{10,... | collective-permute-start | bytes 239624 | tf_op jit(solution)/shard_map/ppermute | solution.py:373
  17.7 0.0 collective-permute-done.3.refs_7_
  17.7 0.0 collective-permute-start.7
  17.7 0.0 collective-permute-done.2.refs_6_
  17.7 0.5 %collective-permute-start.6 = (bf16[48,1664]{1,0:T(8,128)(2,1)S(1)}, bf16[48,1664]{1,0:T(8,128)(2,1)S(1)}, u32[]{:S(2)}, u32[]{:S(2)}) collective-permute-start(bf16[48,1664]{1,0:T(8,128)(2,1)S(1)} %collective-permute-done.2.refs_6_), channel_id=1, source_target_pairs={{0,1},{1,0},{2,3},{3,2},{4,5},{5,4},{6,7},{7,6},{8,9},{9,8},{10,11... | collective-permute-start | bytes 479240 | tf_op jit(solution)/shard_map/ppermute | solution.py:375
  18.2 0.1 collective-permute-start.4
  18.3 2.3 %collective-permute-done.1.refs_5_ = bf16[24,1664]{1,0:T(8,128)(2,1)S(1)} collective-permute-done((bf16[24,1664]{1,0:T(8,128)(2,1)S(1)}, bf16[24,1664]{1,0:T(8,128)(2,1)S(1)}, u32[]{:S(2)}, u32[]{:S(2)}) %collective-permute-start.1) | collective-permute-done | bytes 79904 | tf_op jit(solution)/shard_map/ppermute | solution.py:373
  20.6 0.0 collective-permute-start.5
  20.6 3.4 %prepare.1 = (f32[192,1664]{1,0:T(8,128)S(1)}, f32[192,1664]{1,0:T(8,128)S(1)}, bf16[192,1664]{1,0:T(8,128)(2,1)S(1)}, bf16[192,1664]{1,0:T(8,128)(2,1)S(1)}, f3...) custom-call(f32[192,1664]{1,0:T(8,128)} %refs_0_.2, ...), custom_call_target="tpu_custom_call" | custom-call | tf_op jit(solution)/shard_map/prepare/pallas_call | solution.py:391
  24.0 0.0 collective-permute-done.4.refs_8_
  24.0 0.0 collective-permute-done.5.refs_9_
  24.0 0.0 collective-permute-done.7.refs_11_
  24.0 0.0 collective-permute-done.6.refs_10_
  24.0 0.0 copy-done
  24.0 0.0 copy-done.1
  24.0 0.0 copy-done.2
  24.1 2.6 %update.1 = (f32[192,1664]{1,0:T(8,128)S(1)}, f32[192,1664]{1,0:T(8,128)S(1)}, f32[32,128]{1,0:T(8,128)S(1)}) custom-call(s32[16]{0:T(128)S(1)} %copy-done.2, f32[2,8,128]{2,1,0:T(8,128)S(1)} %get-tuple-element.17.refs_1_, bf16[48,1664]{1,0:T(8,128)(2,1)S(1)} %copy-done, bf16[48,1664]{1,0:T(8,128)(2,1)S(1)} %copy-done.1, ...), custom_call_target="tpu_custom_call" | custom-call | tf_op jit(solution)/shard_map/update/pallas_call | solution.py:394
  26.7 12.5 %all_to_all.11 = f32[32,1,128]{2,1,0:T(1,128)S(1)} all-to-all(f32[32,1,128]{2,1,0:T(1,128)S(1)} %bitcast.5), channel_id=1, replica_groups=mesh['dp'=4,'mp'=8] {'dp','mp'}, dimensions={0} | all-to-all | bytes 32768 | tf_op jit(solution)/shard_map/all_to_all | solution.py:406
  39.1 1.7 %finish.1 = (f32[192,1664]{1,0:T(8,128)}, f32[192,1664]{1,0:T(8,128)}, f32[2]{0:T(128)}) custom-call(f32[32,128]{1,0:T(8,128)S(1)} %bitcast.4, f32[192,1664]{1,0:T(8,128)S(1)} %get-tuple-element.27.up_ref, f32[192,1664]{1,0:T(8,128)S(1)} %get-tuple-element.28.down_ref, f32[192,1664]{1,0:T(8,128)S(1)} %get-tuple-element.29.step_up_ref, ...), custom_call_target="tpu_custom_call" | custom-call | tf_op jit(solution)/shard_map/finish/pallas_call | solution.py:408
  (1 shorter events, 0.0 us)
Async XLA Ops:
  1.6 16.1 %collective-permute-start.3 = (bf16[48,1664]{1,0:T(8,128)(2,1)S(1)}, bf16[48,1664]{1,0:T(8,128)(2,1)S(1)}, u32[]{:S(2)}, u32[]{:S(2)}) collective-permute-start(bf16[48,1664]{1,0:T(8,128)(2,1)S(1)} %broadcast_select_fusion), channel_id=1, source_target_pairs={{0,16},{8,24},{16,0},{24,8},{1,17},{9,25},{17,1},{25,9},{2,18},{10... | collective-permute-start | bytes 479240 | tf_op jit(solution)/shard_map/ppermute | solution.py:370
  5.7 12.0 %collective-permute-start.2 = (bf16[48,1664]{1,0:T(8,128)(2,1)S(1)}, bf16[48,1664]{1,0:T(8,128)(2,1)S(1)}, u32[]{:S(2)}, u32[]{:S(2)}) collective-permute-start(bf16[48,1664]{1,0:T(8,128)(2,1)S(1)} %broadcast_select_fusion), channel_id=1, source_target_pairs={{0,8},{8,0},{16,24},{24,16},{1,9},{9,1},{17,25},{25,17},{2,10},{10... | collective-permute-start | bytes 479240 | tf_op jit(solution)/shard_map/ppermute | solution.py:370
  7.3 16.7 %copy-start = (bf16[48,1664]{1,0:T(8,128)(2,1)S(1)}, bf16[48,1664]{1,0:T(8,128)(2,1)}, u32[]{:S(2)}) copy-start(bf16[48,1664]{1,0:T(8,128)(2,1)} %refs_2_.3) | copy-start | bytes 479236
  7.3 16.7 %copy-start.1 = (bf16[48,1664]{1,0:T(8,128)(2,1)S(1)}, bf16[48,1664]{1,0:T(8,128)(2,1)}, u32[]{:S(2)}) copy-start(bf16[48,1664]{1,0:T(8,128)(2,1)} %refs_3_.3) | copy-start | bytes 479236
  7.3 16.7 %copy-start.2 = (s32[16]{0:T(128)S(1)}, s32[16]{0:T(128)}, u32[]{:S(2)}) copy-start(s32[16]{0:T(128)} %refs_0_.3) | copy-start | bytes 196
  7.3 8.8 %collective-permute-start = (bf16[24,1664]{1,0:T(8,128)(2,1)S(1)}, bf16[24,1664]{1,0:T(8,128)(2,1)S(1)}, u32[]{:S(2)}, u32[]{:S(2)}) collective-permute-start(bf16[24,1664]{1,0:T(8,128)(2,1)S(1)} %constant_dynamic-slice_fusion), channel_id=1, source_target_pairs={{0,24},{8,16},{16,8},{24,0},{1,25},{9,17},{17,9},{25,1},{2,26},{10... | collective-permute-start | bytes 239624 | tf_op jit(solution)/shard_map/ppermute | solution.py:370
  16.2 4.4 %collective-permute-start.1 = (bf16[24,1664]{1,0:T(8,128)(2,1)S(1)}, bf16[24,1664]{1,0:T(8,128)(2,1)S(1)}, u32[]{:S(2)}, u32[]{:S(2)}) collective-permute-start(bf16[24,1664]{1,0:T(8,128)(2,1)S(1)} %collective-permute-done.refs_4_), channel_id=1, source_target_pairs={{0,2},{1,3},{2,0},{3,1},{4,6},{5,7},{6,4},{7,5},{8,10},{9,11},{10,... | collective-permute-start | bytes 239624 | tf_op jit(solution)/shard_map/ppermute | solution.py:373
  17.7 6.3 %collective-permute-start.7 = (bf16[48,1664]{1,0:T(8,128)(2,1)S(1)}, bf16[48,1664]{1,0:T(8,128)(2,1)S(1)}, u32[]{:S(2)}, u32[]{:S(2)}) collective-permute-start(bf16[48,1664]{1,0:T(8,128)(2,1)S(1)} %collective-permute-done.3.refs_7_), channel_id=1, source_target_pairs={{0,1},{1,0},{2,3},{3,2},{4,5},{5,4},{6,7},{7,6},{8,9},{9,8},{10,11... | collective-permute-start | bytes 479240 | tf_op jit(solution)/shard_map/ppermute | solution.py:375
  17.7 6.3 %collective-permute-start.6 = (bf16[48,1664]{1,0:T(8,128)(2,1)S(1)}, bf16[48,1664]{1,0:T(8,128)(2,1)S(1)}, u32[]{:S(2)}, u32[]{:S(2)}) collective-permute-start(bf16[48,1664]{1,0:T(8,128)(2,1)S(1)} %collective-permute-done.2.refs_6_), channel_id=1, source_target_pairs={{0,1},{1,0},{2,3},{3,2},{4,5},{5,4},{6,7},{7,6},{8,9},{9,8},{10,11... | collective-permute-start | bytes 479240 | tf_op jit(solution)/shard_map/ppermute | solution.py:375
  18.2 5.8 %collective-permute-start.4 = (bf16[24,1664]{1,0:T(8,128)(2,1)S(1)}, bf16[24,1664]{1,0:T(8,128)(2,1)S(1)}, u32[]{:S(2)}, u32[]{:S(2)}) collective-permute-start(bf16[24,1664]{1,0:T(8,128)(2,1)S(1)} %collective-permute-done.refs_4_), channel_id=1, source_target_pairs={{0,1},{1,0},{2,3},{3,2},{4,5},{5,4},{6,7},{7,6},{8,9},{9,8},{10,11... | collective-permute-start | bytes 239624 | tf_op jit(solution)/shard_map/ppermute | solution.py:375
  20.6 3.4 %collective-permute-start.5 = (bf16[24,1664]{1,0:T(8,128)(2,1)S(1)}, bf16[24,1664]{1,0:T(8,128)(2,1)S(1)}, u32[]{:S(2)}, u32[]{:S(2)}) collective-permute-start(bf16[24,1664]{1,0:T(8,128)(2,1)S(1)} %collective-permute-done.1.refs_5_), channel_id=1, source_target_pairs={{0,1},{1,0},{2,3},{3,2},{4,5},{5,4},{6,7},{7,6},{8,9},{9,8},{10,11... | collective-permute-start | bytes 239624 | tf_op jit(solution)/shard_map/ppermute | solution.py:375

commit v2 on v1

--- a/solution.py
+++ b/solution.py
@@ -193,15 +193,8 @@
         low = slot * cap + half * (cap // 2)
         rows = slice(low, low + far.shape[0])
 
-        @pl.when(core == 0)
-        def _():
-            inputs_ref[rows, :] = far[...]
-            cotangent_ref[rows, :] = near[...]
-
-        @pl.when(core != 0)
-        def _():
-            inputs_ref[rows, :] = near[...]
-            cotangent_ref[rows, :] = far[...]
+        inputs_ref[rows, :] = jnp.where(core == 0, far[...], near[...])
+        cotangent_ref[rows, :] = jnp.where(core == 0, near[...], far[...])
 
     total = patches_ref[0]
     for at in range(1, groups * images):
@@ -307,7 +300,7 @@
             copy = pltpu.make_async_copy(
                 held_ref.at[at, here], new_ref.at[here], sem_ref.at[at, part]
             )
-            copy.start()
+            copy.start(priority=part % 2)
             copies.append(copy)
     copies.append(pltpu.make_async_copy(pair_ref, ratios_ref, pair_sem_ref))
     copies[-1].start()
@@ -413,7 +406,7 @@
         scratch_shapes=[
             pltpu.VMEM((2, rows, width), jnp.float32),
             pltpu.SMEM((2,), jnp.float32),
-            pltpu.SemaphoreType.DMA((2, 6)),
+            pltpu.SemaphoreType.DMA((2, 3)),
             pltpu.SemaphoreType.DMA,
         ],
         compiler_params=pltpu.CompilerParams(vmem_limit_bytes=kernel_room),

time: 41 us -> 41 us (level)
  no operation moved by 1% of the time
where the time goes in v2:
time: 41 us; the launch traced here: 40.8 us
  blocking collectives  12.5 us (30%)
  waiting for transfers between devices  11.1 us (27%)
  starting transfers between devices  7.85 us (19%)
  Pallas kernels  7.64 us (19%)
  other arithmetic  0.95 us (2%)
  between operations  0.75 us (2%)
    all_to_all x1, blocking collectives, gather_tokens(): sums = keep_near(lax.all_to_all(sums, ('dp', 'mp'), 0, 0, tiled=True))  12.5 us
    ppermute x3, waiting for transfers between devices, gather_tokens(): blocks = [lax.ppermute(sent, 'dp', swap)]  8.77 us
    ppermute x3, starting transfers between devices, gather_tokens(): blocks = [lax.ppermute(sent, 'dp', swap)]  5.78 us
    pallas_call x1, Pallas kernels, gather_tokens(): prepare(*(pltpu.with_memory_space_constraint(value, pltpu.HBM) for value...  3.37 us
    pallas_call x1, Pallas kernels, gather_tokens(): pl.pallas_call(functools.partial(update_kernel, groups, devices, hidden_u...  2.54 us
    ppermute x1, waiting for transfers between devices, gather_tokens(): blocks.append(lax.ppermute(blocks[0], 'mp', across))  2.34 us
    pallas_call x1, Pallas kernels, gather_tokens(): pl.pallas_call(finish_kernel, out_shape=(full, full, jax.ShapeDtypeStruct...  1.73 us
    ppermute x1, starting transfers between devices, gather_tokens(): blocks.append(lax.ppermute(blocks[0], 'mp', across))  1.49 us
  transfers between devices with their start and end apart: 8, of which 2 were waited for; matrix products, arithmetic and copies ran while one was open for 0% of the time, Pallas kernels for 8%

profile of v2, /device:TPU:0, one launch (start us, length us, event | category | flops | bytes accessed | tf_op | source)
XLA Modules:
  0.0 40.8 jit_solution(12804322145315650148)
XLA Ops:
  0.6 0.9 %broadcast_select_fusion = bf16[48,1664]{1,0:T(8,128)(2,1)S(1)} fusion(bf16[48,1664]{1,0:T(8,128)(2,1)} %refs_2_.3, bf16[48,1664]{1,0:T(8,128)(2,1)} %refs_3_.3, pred[]{:T(512)S(6)} %eq.6), kind=kLoop, calls=%fused_computation | loop fusion | flops 79872 | bytes 479233 | tf_op jit(solution)/shard_map/jit(_where)/select_n | solution.py:353
  1.6 4.1 %collective-permute-start.3 = (bf16[48,1664]{1,0:T(8,128)(2,1)S(1)}, bf16[48,1664]{1,0:T(8,128)(2,1)S(1)}, u32[]{:S(2)}, u32[]{:S(2)}) collective-permute-start(bf16[48,1664]{1,0:T(8,128)(2,1)S(1)} %broadcast_select_fusion), channel_id=1, source_target_pairs={{0,16},{8,24},{16,0},{24,8},{1,17},{9,25},{17,1},{25,9},{2,18},{10... | collective-permute-start | bytes 479240 | tf_op jit(solution)/shard_map/ppermute | solution.py:363
  5.7 1.6 %collective-permute-start.2 = (bf16[48,1664]{1,0:T(8,128)(2,1)S(1)}, bf16[48,1664]{1,0:T(8,128)(2,1)S(1)}, u32[]{:S(2)}, u32[]{:S(2)}) collective-permute-start(bf16[48,1664]{1,0:T(8,128)(2,1)S(1)} %broadcast_select_fusion), channel_id=1, source_target_pairs={{0,8},{8,0},{16,24},{24,16},{1,9},{9,1},{17,25},{25,17},{2,10},{10... | collective-permute-start | bytes 479240 | tf_op jit(solution)/shard_map/ppermute | solution.py:363
  7.3 0.0 copy-start
  7.3 0.0 copy-start.1
  7.3 0.0 copy-start.2
  7.3 0.1 collective-permute-start
  7.4 8.8 %collective-permute-done.refs_4_ = bf16[24,1664]{1,0:T(8,128)(2,1)S(1)} collective-permute-done((bf16[24,1664]{1,0:T(8,128)(2,1)S(1)}, bf16[24,1664]{1,0:T(8,128)(2,1)S(1)}, u32[]{:S(2)}, u32[]{:S(2)}) %collective-permute-start) | collective-permute-done | bytes 79904 | tf_op jit(solution)/shard_map/ppermute | solution.py:363
  16.2 1.5 %collective-permute-start.1 = (bf16[24,1664]{1,0:T(8,128)(2,1)S(1)}, bf16[24,1664]{1,0:T(8,128)(2,1)S(1)}, u32[]{:S(2)}, u32[]{:S(2)}) collective-permute-start(bf16[24,1664]{1,0:T(8,128)(2,1)S(1)} %collective-permute-done.refs_4_), channel_id=1, source_target_pairs={{0,2},{1,3},{2,0},{3,1},{4,6},{5,7},{6,4},{7,5},{8,10},{9,11},{10,... | collective-permute-start | bytes 239624 | tf_op jit(solution)/shard_map/ppermute | solution.py:366
  17.7 0.0 collective-permute-done.3.refs_7_
  17.7 0.0 collective-permute-start.7
  17.7 0.0 collective-permute-done.2.refs_6_
  17.7 0.5 %collective-permute-start.6 = (bf16[48,1664]{1,0:T(8,128)(2,1)S(1)}, bf16[48,1664]{1,0:T(8,128)(2,1)S(1)}, u32[]{:S(2)}, u32[]{:S(2)}) collective-permute-start(bf16[48,1664]{1,0:T(8,128)(2,1)S(1)} %collective-permute-done.2.refs_6_), channel_id=1, source_target_pairs={{0,1},{1,0},{2,3},{3,2},{4,5},{5,4},{6,7},{7,6},{8,9},{9,8},{10,11... | collective-permute-start | bytes 479240 | tf_op jit(solution)/shard_map/ppermute | solution.py:368
  18.2 0.1 collective-permute-start.4
  18.3 2.3 %collective-permute-done.1.refs_5_ = bf16[24,1664]{1,0:T(8,128)(2,1)S(1)} collective-permute-done((bf16[24,1664]{1,0:T(8,128)(2,1)S(1)}, bf16[24,1664]{1,0:T(8,128)(2,1)S(1)}, u32[]{:S(2)}, u32[]{:S(2)}) %collective-permute-start.1) | collective-permute-done | bytes 79904 | tf_op jit(solution)/shard_map/ppermute | solution.py:366
  20.6 0.0 collective-permute-start.5
  20.6 3.4 %prepare.1 = (f32[192,1664]{1,0:T(8,128)S(1)}, f32[192,1664]{1,0:T(8,128)S(1)}, bf16[192,1664]{1,0:T(8,128)(2,1)S(1)}, bf16[192,1664]{1,0:T(8,128)(2,1)S(1)}, f3...) custom-call(f32[192,1664]{1,0:T(8,128)} %refs_0_.2, ...), custom_call_target="tpu_custom_call" | custom-call | tf_op jit(solution)/shard_map/prepare/pallas_call | solution.py:384
  24.0 0.0 collective-permute-done.4.refs_8_
  24.0 0.0 collective-permute-done.5.refs_9_
  24.0 0.0 collective-permute-done.7.refs_11_
  24.0 0.0 collective-permute-done.6.refs_10_
  24.0 0.0 copy-done
  24.0 0.0 copy-done.1
  24.0 0.0 copy-done.2
  24.1 2.5 %update.1 = (f32[192,1664]{1,0:T(8,128)S(1)}, f32[192,1664]{1,0:T(8,128)S(1)}, f32[32,128]{1,0:T(8,128)S(1)}) custom-call(s32[16]{0:T(128)S(1)} %copy-done.2, f32[2,8,128]{2,1,0:T(8,128)S(1)} %get-tuple-element.17.refs_1_, bf16[48,1664]{1,0:T(8,128)(2,1)S(1)} %copy-done, bf16[48,1664]{1,0:T(8,128)(2,1)S(1)} %copy-done.1, ...), custom_call_target="tpu_custom_call" | custom-call | tf_op jit(solution)/shard_map/update/pallas_call | solution.py:387
  26.6 12.5 %all_to_all.11 = f32[32,1,128]{2,1,0:T(1,128)S(1)} all-to-all(f32[32,1,128]{2,1,0:T(1,128)S(1)} %bitcast.5), channel_id=1, replica_groups=mesh['dp'=4,'mp'=8] {'dp','mp'}, dimensions={0} | all-to-all | bytes 32768 | tf_op jit(solution)/shard_map/all_to_all | solution.py:399
  39.1 1.7 %finish.1 = (f32[192,1664]{1,0:T(8,128)}, f32[192,1664]{1,0:T(8,128)}, f32[2]{0:T(128)}) custom-call(f32[32,128]{1,0:T(8,128)S(1)} %bitcast.4, f32[192,1664]{1,0:T(8,128)S(1)} %get-tuple-element.27.up_ref, f32[192,1664]{1,0:T(8,128)S(1)} %get-tuple-element.28.down_ref, f32[192,1664]{1,0:T(8,128)S(1)} %get-tuple-element.29.step_up_ref, ...), custom_call_target="tpu_custom_call" | custom-call | tf_op jit(solution)/shard_map/finish/pallas_call | solution.py:401
  (1 shorter events, 0.0 us)
Async XLA Ops:
  1.6 16.1 %collective-permute-start.3 = (bf16[48,1664]{1,0:T(8,128)(2,1)S(1)}, bf16[48,1664]{1,0:T(8,128)(2,1)S(1)}, u32[]{:S(2)}, u32[]{:S(2)}) collective-permute-start(bf16[48,1664]{1,0:T(8,128)(2,1)S(1)} %broadcast_select_fusion), channel_id=1, source_target_pairs={{0,16},{8,24},{16,0},{24,8},{1,17},{9,25},{17,1},{25,9},{2,18},{10... | collective-permute-start | bytes 479240 | tf_op jit(solution)/shard_map/ppermute | solution.py:363
  5.7 12.0 %collective-permute-start.2 = (bf16[48,1664]{1,0:T(8,128)(2,1)S(1)}, bf16[48,1664]{1,0:T(8,128)(2,1)S(1)}, u32[]{:S(2)}, u32[]{:S(2)}) collective-permute-start(bf16[48,1664]{1,0:T(8,128)(2,1)S(1)} %broadcast_select_fusion), channel_id=1, source_target_pairs={{0,8},{8,0},{16,24},{24,16},{1,9},{9,1},{17,25},{25,17},{2,10},{10... | collective-permute-start | bytes 479240 | tf_op jit(solution)/shard_map/ppermute | solution.py:363
  7.3 16.7 %copy-start = (bf16[48,1664]{1,0:T(8,128)(2,1)S(1)}, bf16[48,1664]{1,0:T(8,128)(2,1)}, u32[]{:S(2)}) copy-start(bf16[48,1664]{1,0:T(8,128)(2,1)} %refs_2_.3) | copy-start | bytes 479236
  7.3 16.7 %copy-start.1 = (bf16[48,1664]{1,0:T(8,128)(2,1)S(1)}, bf16[48,1664]{1,0:T(8,128)(2,1)}, u32[]{:S(2)}) copy-start(bf16[48,1664]{1,0:T(8,128)(2,1)} %refs_3_.3) | copy-start | bytes 479236
  7.3 16.7 %copy-start.2 = (s32[16]{0:T(128)S(1)}, s32[16]{0:T(128)}, u32[]{:S(2)}) copy-start(s32[16]{0:T(128)} %refs_0_.3) | copy-start | bytes 196
  7.3 8.8 %collective-permute-start = (bf16[24,1664]{1,0:T(8,128)(2,1)S(1)}, bf16[24,1664]{1,0:T(8,128)(2,1)S(1)}, u32[]{:S(2)}, u32[]{:S(2)}) collective-permute-start(bf16[24,1664]{1,0:T(8,128)(2,1)S(1)} %constant_dynamic-slice_fusion), channel_id=1, source_target_pairs={{0,24},{8,16},{16,8},{24,0},{1,25},{9,17},{17,9},{25,1},{2,26},{10... | collective-permute-start | bytes 239624 | tf_op jit(solution)/shard_map/ppermute | solution.py:363
  16.2 4.4 %collective-permute-start.1 = (bf16[24,1664]{1,0:T(8,128)(2,1)S(1)}, bf16[24,1664]{1,0:T(8,128)(2,1)S(1)}, u32[]{:S(2)}, u32[]{:S(2)}) collective-permute-start(bf16[24,1664]{1,0:T(8,128)(2,1)S(1)} %collective-permute-done.refs_4_), channel_id=1, source_target_pairs={{0,2},{1,3},{2,0},{3,1},{4,6},{5,7},{6,4},{7,5},{8,10},{9,11},{10,... | collective-permute-start | bytes 239624 | tf_op jit(solution)/shard_map/ppermute | solution.py:366
  17.7 6.3 %collective-permute-start.7 = (bf16[48,1664]{1,0:T(8,128)(2,1)S(1)}, bf16[48,1664]{1,0:T(8,128)(2,1)S(1)}, u32[]{:S(2)}, u32[]{:S(2)}) collective-permute-start(bf16[48,1664]{1,0:T(8,128)(2,1)S(1)} %collective-permute-done.3.refs_7_), channel_id=1, source_target_pairs={{0,1},{1,0},{2,3},{3,2},{4,5},{5,4},{6,7},{7,6},{8,9},{9,8},{10,11... | collective-permute-start | bytes 479240 | tf_op jit(solution)/shard_map/ppermute | solution.py:368
  17.7 6.3 %collective-permute-start.6 = (bf16[48,1664]{1,0:T(8,128)(2,1)S(1)}, bf16[48,1664]{1,0:T(8,128)(2,1)S(1)}, u32[]{:S(2)}, u32[]{:S(2)}) collective-permute-start(bf16[48,1664]{1,0:T(8,128)(2,1)S(1)} %collective-permute-done.2.refs_6_), channel_id=1, source_target_pairs={{0,1},{1,0},{2,3},{3,2},{4,5},{5,4},{6,7},{7,6},{8,9},{9,8},{10,11... | collective-permute-start | bytes 479240 | tf_op jit(solution)/shard_map/ppermute | solution.py:368
  18.2 5.8 %collective-permute-start.4 = (bf16[24,1664]{1,0:T(8,128)(2,1)S(1)}, bf16[24,1664]{1,0:T(8,128)(2,1)S(1)}, u32[]{:S(2)}, u32[]{:S(2)}) collective-permute-start(bf16[24,1664]{1,0:T(8,128)(2,1)S(1)} %collective-permute-done.refs_4_), channel_id=1, source_target_pairs={{0,1},{1,0},{2,3},{3,2},{4,5},{5,4},{6,7},{7,6},{8,9},{9,8},{10,11... | collective-permute-start | bytes 239624 | tf_op jit(solution)/shard_map/ppermute | solution.py:368
  20.6 3.4 %collective-permute-start.5 = (bf16[24,1664]{1,0:T(8,128)(2,1)S(1)}, bf16[24,1664]{1,0:T(8,128)(2,1)S(1)}, u32[]{:S(2)}, u32[]{:S(2)}) collective-permute-start(bf16[24,1664]{1,0:T(8,128)(2,1)S(1)} %collective-permute-done.1.refs_5_), channel_id=1, source_target_pairs={{0,1},{1,0},{2,3},{3,2},{4,5},{5,4},{6,7},{7,6},{8,9},{9,8},{10,11... | collective-permute-start | bytes 239624 | tf_op jit(solution)/shard_map/ppermute | solution.py:368
